TPU v7x, 32 devices: a whole 2x2x4 slice. The times are simulated.
32 devices in a mesh: wide: 8 (over z, y), narrow: 4 (over x, core).
Axes of the slice: x: 2, y: 2, z: 4, core: 2. Of those that a mesh axis runs over, the one named last changes fastest.
Arguments:
- frames: float32 [32768, 440], P(('wide', 'narrow')), may hold values from -8 to 8
- targets: float32 [32768, 2048], P(('wide', 'narrow')), may hold values from -7 to 7
- projection: float32 [32, 440, 512], P(('wide', 'narrow')), may hold values from -0.25 to 0.25
- phases: float32 [32, 512], P(('wide', 'narrow')), may hold values from 0 to 6.283185
- block_order: int32 [32], replicated, may hold values from 0 to 31, each once
Outputs:
- residual: float32 [32768, 2048], P(('wide', 'narrow'))
- weights: float32 [2, 512, 2048], replicated
Inputs may be any that keep to these rules, and one draw needn't show every extreme that they name: `block_order`: a permutation; steps use its first 2 entries.
All inputs are finite; a program needn't handle non-finite values.
Results may differ from a plain program's by a relative error of at most 0.0003.
Values sent between devices are 32-bit elements; how exact they have to be, the bound alone decides.
No kernel may reach another device: no remote copies, remote signals or barrier semaphores. Data moves between devices by JAX's collectives and lax.ppermute only.
A program may use at most 128 MiB of HBM per device.

v0:
```python
import jax
import jax.numpy as jnp
from jax import lax
from jax.sharding import PartitionSpec as P

STEPS = 2


def from_root(value, axis, source):
    kept = jnp.where(lax.axis_index(axis) == source, value, 0).astype(value.dtype)
    return lax.psum(kept, axis)


def features_of(frames, block_proj, block_phase):
    inner = jnp.dot(
        frames, block_proj, precision=lax.Precision.HIGHEST, preferred_element_type=jnp.float32
    )
    return jnp.sqrt(2.0 / block_proj.shape[1]) * jnp.cos(inner + block_phase[None, :])


def local_product(left, right):
    return jnp.dot(
        left.T, right, precision=lax.Precision.HIGHEST, preferred_element_type=jnp.float32
    )


def solve_block(gram_sum, cross_sum):
    width = gram_sum.shape[0]
    damping = 0.1 * jnp.trace(gram_sum) / width
    factor = jnp.linalg.cholesky(gram_sum + damping * jnp.eye(width, dtype=gram_sum.dtype))
    return jax.scipy.linalg.cho_solve((factor, True), cross_sum)


def per_device(frames, targets, projection, phases, block_order):
    feature_list = []
    for step_index in range(STEPS):
        block_proj, block_phase = (
            from_root(projection, ("wide", "narrow"), block_order[step_index]),
            from_root(phases, ("wide", "narrow"), block_order[step_index]),
        )
        feature_list.append(features_of(frames, block_proj[0], block_phase[0]))
    residual = targets
    solved = []
    for step_index in range(STEPS):
        feats = feature_list[step_index]
        cross_local = local_product(feats, residual)
        gram_sum = lax.psum(local_product(feats, feats), ("wide", "narrow"))
        cross_share = lax.psum_scatter(cross_local, "narrow", scatter_dimension=1, tiled=True)
        cross_share = lax.psum(cross_share, "wide")
        weight_share = solve_block(gram_sum, cross_share)
        weights = lax.all_gather(weight_share, "narrow", axis=1, tiled=True)
        residual = residual - jnp.dot(
            feats, weights, precision=lax.Precision.HIGHEST, preferred_element_type=jnp.float32
        )
        solved.append(weights)
    return (residual, jnp.stack(solved))


def solution(mesh):
    return jax.shard_map(
        per_device,
        mesh=mesh,
        in_specs=(
            P(("wide", "narrow"), None),
            P(("wide", "narrow"), None),
            P(("wide", "narrow"), None, None),
            P(("wide", "narrow"), None),
            P(),
        ),
        out_specs=(P(("wide", "narrow"), None), P()),
        check_vma=False,
    )
```

profile of v0, /device:TPU:0, one launch (start us, length us, event | category | flops | bytes accessed | tf_op | source)
XLA Modules:
  0.0 830.9 jit_solution(9541933310264790107)
XLA Ops:
  12.6 42.1 %all-reduce.1 = (f32[512]{0:T(512)S(1)}, f32[512]{0:T(512)S(1)}) all-reduce(f32[512]{0:T(512)S(1)} %bitcast.143, f32[512]{0:T(512)S(1)} %bitcast.142), channel_id=1, replica_groups=mesh['wide'=8,'narrow'=4] {'wide','narrow'}, use_global_device_ids=true, to_apply=%region_1.2 | all-reduce | flops 1024 | bytes 8192 | tf_op jit(solution)/shard_map/psum | solution.py:11
  54.7 96.0 %all-reduce.15.cloned.1.call-done = (f32[440,512]{1,0:T(8,128)}, f32[440,512]{1,0:T(8,128)}) async-done(((f32[440,512]{1,0:T(8,128)}, f32[440,512]{1,0:T(8,128)}), (f32[440,512]{1,0:T(8,128)}, f32[440,512]{1,0:T(8,128)})) %all-reduce.15.cloned.1.call-update) | async-done | bytes 1802256 | tf_op jit(solution)/shard_map/psum | solution.py:11
  150.7 11.2 %cosine_multiply_fusion.1 = f32[512,1024]{1,0:T(8,128)S(1)} fusion(f32[440,512]{1,0:T(8,128)} %get-tuple-element.40, f32[1024,440]{0,1:T(8,128)S(1)} %copy-done, f32[512]{0:T(512)S(1)} %get-tuple-element.36), kind=kOutput, calls=%fused_computation.8 | convolution fusion | flops 2769289216 | bytes 4802560 | tf_op jit(solution)/shard_map/dot_general | solution.py:15
  162.0 13.4 %fusion.97 = f32[512,512]{0,1:T(8,128)} fusion(f32[512,1024]{1,0:T(8,128)S(1)} %cosine_multiply_fusion.1), kind=kOutput, calls=%fused_computation.185 | convolution fusion | flops 3221225472 | bytes 3145728 | tf_op jit(solution)/shard_map/dot_general | solution.py:22
  191.7 18.0 %fusion.98 = f32[512,2048]{1,0:T(8,128)} fusion(f32[512,1024]{1,0:T(8,128)} %copy-done.5, f32[1024,2048]{1,0:T(8,128)} %param.9), kind=kOutput, calls=%fused_computation.186 | convolution fusion | flops 12884901888 | bytes 14680064 | tf_op jit(solution)/shard_map/dot_general | solution.py:22
  210.2 115.3 %all-reduce.13.cloned.1.call-done = (f32[512,512]{0,1:T(8,128)}, f32[512,512]{0,1:T(8,128)}) async-done(((f32[512,512]{0,1:T(8,128)}, f32[512,512]{0,1:T(8,128)}), (f32[512,512]{0,1:T(8,128)}, f32[512,512]{0,1:T(8,128)})) %all-reduce.13.cloned.1.call-update) | async-done | bytes 2097168 | tf_op jit(solution)/shard_map/psum | solution.py:47
  336.4 11.7 %cholesky.286 = f32[128,128]{1,0:T(8,128)S(1)} custom-call(f32[128,128]{1,0:T(8,128)S(1)} %cholesky.426), custom_call_target="Cholesky" | custom-call | tf_op jit(solution)/shard_map/jit(cholesky)/cholesky | solution.py:30
  360.6 11.7 %cholesky.305 = f32[128,128]{1,0:T(8,128)S(1)} custom-call(f32[128,128]{1,0:T(8,128)S(1)} %cholesky.430), custom_call_target="Cholesky" | custom-call | tf_op jit(solution)/shard_map/jit(cholesky)/cholesky | solution.py:30
  383.9 11.7 %cholesky.326 = f32[128,128]{1,0:T(8,128)S(1)} custom-call(f32[128,128]{1,0:T(8,128)S(1)} %cholesky.435), custom_call_target="Cholesky" | custom-call | tf_op jit(solution)/shard_map/jit(cholesky)/cholesky | solution.py:30
  406.9 11.9 %cholesky.343 = f32[128,128]{1,0:T(8,128)S(1)} custom-call(f32[128,128]{1,0:T(8,128)S(1)} %convolution_subtract_fusion.19), custom_call_target="Cholesky" | custom-call | tf_op jit(solution)/shard_map/jit(cholesky)/cholesky | solution.py:30
  425.5 11.8 %while.4 = (s32[]{:T(128)}, f32[512,512]{1,0:T(8,128)}, s32[4,2]{0,1:T(2,128)S(1)}, f32[4,128,128]{2,1,0:T(8,128)S(1)}, s32[]{:T(128)}) while((s32[]{:T(128)}, f32[512,512]{1,0:T(8,128)}, s32[4,2]{0,1:T(2,128)S(1)}, f32[4,128,128]{2,1,0:T(8,128)S(1)}, s32[]{:T(128)}) %tuple.58), condition=%wide.while_cond, body=%wide.while_body.sunk | while | flops 2 | bytes 131189 | solution.py:31
  437.3 39.3 %custom-call.32 = f32[4,128,128]{1,2,0:T(8,128)S(1)} custom-call(f32[4,128,128]{2,1,0:T(8,128)S(1)} %get-tuple-element.18), custom_call_target="InvertDiagBlocksLowerTriangular" | custom-call | tf_op jit(solution)/shard_map/jit(_cho_solve)/triangular_solve | solution.py:31
  476.6 26.8 %all-reduce.9.cloned.1.call-done = f32[512,512]{1,0:T(8,128)} async-done(((f32[512,512]{1,0:T(8,128)}), f32[512,512]{1,0:T(8,128)}) %all-reduce.9.cloned.1.call-update) | async-done | bytes 1048592 | tf_op jit(solution)/shard_map/psum | solution.py:49
  515.0 33.7 %all-gather.3.cloned.1.call-done = f32[512,2048]{1,0:T(8,128)} async-done(((f32[512,512]{1,0:T(8,128)}), f32[512,2048]{1,0:T(8,128)}) %all-gather.3.cloned.1.call-update) | async-done | bytes 4194320 | tf_op jit(solution)/shard_map/all_gather | solution.py:51
  548.8 16.9 %convolution_subtract_fusion.1 = f32[1024,2048]{1,0:T(8,128)S(1)} fusion(f32[1024,2048]{1,0:T(8,128)} %param.9, f32[512,1024]{1,0:T(8,128)} %copy-done.5, f32[512,2048]{1,0:T(8,128)} %all-gather.3.cloned.1.call-done), kind=kOutput, calls=%fused_computation.6 | convolution fusion | flops 12886999040 | bytes 23068672 | tf_op jit(solution)/shard_map/dot_general | solution.py:52
  569.1 17.2 %fusion.100 = f32[512,2048]{1,0:T(8,128)} fusion(f32[512,1024]{1,0:T(8,128)} %copy-done.3, f32[1024,2048]{1,0:T(8,128)S(1)} %convolution_subtract_fusion.1), kind=kOutput, calls=%fused_computation.188 | convolution fusion | flops 12884901888 | bytes 14680064 | tf_op jit(solution)/shard_map/dot_general | solution.py:22
  588.1 11.7 %cholesky.358 = f32[128,128]{1,0:T(8,128)S(1)} custom-call(f32[128,128]{1,0:T(8,128)S(1)} %cholesky.439), custom_call_target="Cholesky" | custom-call | tf_op jit(solution)/shard_map/jit(cholesky)/cholesky | solution.py:30
  612.3 11.7 %cholesky.377 = f32[128,128]{1,0:T(8,128)S(1)} custom-call(f32[128,128]{1,0:T(8,128)S(1)} %cholesky.443), custom_call_target="Cholesky" | custom-call | tf_op jit(solution)/shard_map/jit(cholesky)/cholesky | solution.py:30
  635.7 11.7 %cholesky.398 = f32[128,128]{1,0:T(8,128)S(1)} custom-call(f32[128,128]{1,0:T(8,128)S(1)} %cholesky.448), custom_call_target="Cholesky" | custom-call | tf_op jit(solution)/shard_map/jit(cholesky)/cholesky | solution.py:30
  658.7 11.7 %cholesky.415 = f32[128,128]{1,0:T(8,128)S(1)} custom-call(f32[128,128]{1,0:T(8,128)S(1)} %convolution_subtract_fusion.18), custom_call_target="Cholesky" | custom-call | tf_op jit(solution)/shard_map/jit(cholesky)/cholesky | solution.py:30
  684.2 39.3 %custom-call.36 = f32[4,128,128]{1,2,0:T(8,128)S(1)} custom-call(f32[4,128,128]{2,1,0:T(8,128)S(1)} %get-tuple-element.19), custom_call_target="InvertDiagBlocksLowerTriangular" | custom-call | tf_op jit(solution)/shard_map/jit(_cho_solve)/triangular_solve | solution.py:31
  723.5 31.3 %all-reduce.11.cloned.1.call-done = f32[512,512]{1,0:T(8,128)} async-done(((f32[512,512]{1,0:T(8,128)}), f32[512,512]{1,0:T(8,128)}) %all-reduce.11.cloned.1.call-update) | async-done | bytes 1048592 | tf_op jit(solution)/shard_map/psum | solution.py:49
  764.2 34.2 %all-gather.5.cloned.1.call-done = f32[512,2048]{1,0:T(8,128)} async-done(((f32[512,512]{1,0:T(8,128)}), f32[512,2048]{1,0:T(8,128)}) %all-gather.5.cloned.1.call-update) | async-done | bytes 4194320 | tf_op jit(solution)/shard_map/all_gather | solution.py:51
  806.5 17.1 %convolution_subtract_fusion = f32[1024,2048]{1,0:T(8,128)} fusion(f32[1024,2048]{1,0:T(8,128)} %copy-done.2, f32[512,1024]{1,0:T(8,128)S(1)} %copy-done.4, f32[512,2048]{1,0:T(8,128)S(1)} %copy-done.6), kind=kOutput, calls=%fused_computation.5 | convolution fusion | flops 12886999040 | bytes 23068672 | tf_op jit(solution)/shard_map/dot_general | solution.py:52
  (160 shorter events, 170.0 us)
Async XLA Ops:
  7.2 143.5 %copy-start = (f32[1024,440]{0,1:T(8,128)S(1)}, f32[1024,440]{0,1:T(8,128)}, u32[]{:S(2)}) copy-start(f32[1024,440]{0,1:T(8,128)} %param.8) | copy-start | bytes 5406724
  7.2 143.5 %all-reduce.15.cloned.1.call-start = ((), (), s32[]{:S(2)}) async-start(), calls=%async_computation.9 | async-start | bytes 3604480 | tf_op jit(solution)/shard_map/psum | solution.py:11
  9.9 2.7 copy-start.12
  12.6 312.9 %all-reduce.13.cloned.1.call-start = ((), (), s32[]{:S(2)}) async-start(), calls=%async_computation.8 | async-start | bytes 4194304 | tf_op jit(solution)/shard_map/psum | solution.py:47
  161.9 13.4 %copy-start.5 = (f32[512,1024]{1,0:T(8,128)}, f32[512,1024]{1,0:T(8,128)S(1)}, u32[]{:S(2)}) copy-start(f32[512,1024]{1,0:T(8,128)S(1)} %cosine_multiply_fusion.1) | copy-start | bytes 6291460
  162.0 13.4 %copy-start.11 = (f32[440,512]{1,0:T(8,128)S(1)}, f32[440,512]{1,0:T(8,128)}, u32[]{:S(2)}) copy-start(f32[440,512]{1,0:T(8,128)} %get-tuple-element.41) | copy-start | bytes 2703364
  185.7 1.4 copy-start.3
  191.6 233.8 %reduce-scatter.3.cloned.1.call-start = ((), (), s32[]{:S(2)}) async-start(), calls=%async_computation.2 | async-start | bytes 5242880 | tf_op jit(solution)/shard_map/reduce_scatter | solution.py:48
  209.7 293.7 %all-reduce.9.cloned.1.call-start = ((), (), s32[]{:S(2)}) async-start(), calls=%async_computation.3 | async-start | bytes 2097152 | tf_op jit(solution)/shard_map/psum | solution.py:49
  335.4 1.0 copy-start.8
  425.4 123.4 %all-gather.3.cloned.1.call-start = ((), (), s32[]{:S(2)}) async-start(), calls=%async_computation.4 | async-start | bytes 5242880 | tf_op jit(solution)/shard_map/all_gather | solution.py:51
  437.3 69.3 %copy-start.7 = (f32[512,512]{1,0:T(8,128)S(1)}, f32[512,512]{1,0:T(8,128)}, u32[]{:S(2)}) copy-start(f32[512,512]{1,0:T(8,128)} %get-tuple-element.187) | copy-start | bytes 3145732
  514.6 161.5 %reduce-scatter.5.cloned.1.call-start = ((), (), s32[]{:S(2)}) async-start(), calls=%async_computation.5 | async-start | bytes 5242880 | tf_op jit(solution)/shard_map/reduce_scatter | solution.py:48
  565.7 3.4 copy-start.2
  586.3 168.6 %all-reduce.11.cloned.1.call-start = ((), (), s32[]{:S(2)}) async-start(), calls=%async_computation.6 | async-start | bytes 2097152 | tf_op jit(solution)/shard_map/psum | solution.py:49
  587.1 1.0 copy-start.9
  676.1 122.3 %all-gather.5.cloned.1.call-start = ((), (), s32[]{:S(2)}) async-start(), calls=%async_computation.7 | async-start | bytes 5242880 | tf_op jit(solution)/shard_map/all_gather | solution.py:51
  754.9 3.2 copy-start.10
  798.4 8.1 copy-start.4
  798.4 8.1 copy-start.6
  806.5 17.2 %copy-start.1 = (f32[1024,440]{0,1:T(8,128)S(1)}, f32[1024,440]{0,1:T(8,128)}, u32[]{:S(2)}) copy-start(f32[1024,440]{0,1:T(8,128)} %param.8) | copy-start | bytes 5406724
Sparse Core Ops, SparseCore 0:
  14.0 136.6 all-reduce.14
  191.7 133.7 all-reduce.12
  328.6 43.2 reduce-scatter.2
  425.5 77.8 all-reduce.8
  514.7 34.0 all-gather.2
  586.4 44.4 reduce-scatter.4
  676.2 78.6 all-reduce.10
  764.3 34.0 all-gather.4
where the time goes:
time: 841 us; the launch traced here: 831 us
  waiting for transfers between devices  338 us (40%)
  other arithmetic  259 us (31%)
  matrix products  138 us (16%)
  blocking collectives  42.1 us (5%)
  local copies, waits for them, and re-layouts  29.9 us (4%)
  between operations  23 us (3%)
    another operation x30, other arithmetic, solve_block(): jnp.linalg.cholesky(gram_sum + damping * jnp.eye(width, dtype=gram_sum.dt...  159 us
    psum x1, waiting for transfers between devices, per_device(): gram_sum = lax.psum(local_product(feats, feats), ('wide', 'narrow'))  115 us
    psum x1, waiting for transfers between devices, from_root(): return lax.psum(kept, axis)  96 us
    another operation x7, other arithmetic, solve_block(): return jax.scipy.linalg.cho_solve((factor, True), cross_sum)  82.2 us
    all_gather x2, waiting for transfers between devices, per_device(): weights = lax.all_gather(weight_share, 'narrow', axis=1, tiled=True)  68 us
    psum x2, waiting for transfers between devices, per_device(): cross_share = lax.psum(cross_share, 'wide')  58.2 us
    dot_general x4, matrix products, local_product(): jnp.dot(left.T, right, precision=lax.Precision.HIGHEST, preferred_element...  53.1 us
    psum x1, blocking collectives, from_root(): return lax.psum(kept, axis)  42.1 us
  transfers between devices with their start and end apart: 8, of which 6 were waited for; matrix products, arithmetic and copies ran while one was open for 36% of the time, Pallas kernels for 0%

commit v1 on v0

--- a/solution.py
+++ b/solution.py
@@ -4,6 +4,23 @@
 from jax.sharding import PartitionSpec as P
 
 STEPS = 2
+
+
+def in_order(blocks, dim):
+    shape = list(blocks.shape[1:])
+    shape[dim] *= blocks.shape[0]
+    return jnp.moveaxis(blocks, 0, dim).reshape(shape)
+
+
+def doubled(value, axis):
+    size, index = (lax.axis_size(axis), lax.axis_index(axis))
+    blocks, apart = (value[None], 1)
+    while apart < size:
+        theirs = lax.ppermute(blocks, axis, [(i, i ^ apart) for i in range(size)])
+        low = index & apart == 0
+        blocks = jnp.concatenate([jnp.where(low, blocks, theirs), jnp.where(low, theirs, blocks)])
+        apart *= 2
+    return blocks
 
 
 def from_root(value, axis, source):
@@ -48,7 +65,7 @@
         cross_share = lax.psum_scatter(cross_local, "narrow", scatter_dimension=1, tiled=True)
         cross_share = lax.psum(cross_share, "wide")
         weight_share = solve_block(gram_sum, cross_share)
-        weights = lax.all_gather(weight_share, "narrow", axis=1, tiled=True)
+        weights = in_order(doubled(weight_share, "narrow"), 1)
         residual = residual - jnp.dot(
             feats, weights, precision=lax.Precision.HIGHEST, preferred_element_type=jnp.float32
         )

time: 841 us -> 916 us (1.089)
  waiting for transfers between devices: 338 us -> 367 us
  local copies, waits for them, and re-layouts: 29.9 us -> 49.2 us
  matrix products: 138 us -> 155 us
    ppermute x0 -> x4, waiting for transfers between devices: none -> 98.1 us  [doubled(): theirs = lax.ppermute(blocks, axis, [(i, i ^ apart) for i in range(size)])]
    all_gather x2 -> x0, waiting for transfers between devices: 68 us -> none  [per_device(): weights = lax.all_gather(weight_share, 'narrow', axis=1, tiled=True)]
    dot_general x2, matrix products: 34 us -> 60.9 us  [per_device(): jnp.dot(feats, weights, precision=lax.Precision.HIGHEST, preferred_elemen...]
    dot_general x4, matrix products: 53.1 us -> 42.5 us  [local_product(): jnp.dot(left.T, right, precision=lax.Precision.HIGHEST, preferred_element...]
    transpose x0 -> x2, local copies, waits for them, and re-layouts: none -> 10.5 us  [in_order(): return jnp.moveaxis(blocks, 0, dim).reshape(shape)]
    another operation x7 -> x5, other arithmetic: 82.2 us -> 80.1 us  [solve_block(): return jax.scipy.linalg.cho_solve((factor, True), cross_sum)]
  transfers between devices with their start and end apart: 8 -> 10, of which waited for: 6 -> 8; matrix products, arithmetic and copies ran while one was open for 36% -> 33% of each run, Pallas kernels for 0% -> 0%
where the time goes in v1:
time: 916 us; the launch traced here: 906 us
  waiting for transfers between devices  367 us (40%)
  other arithmetic  265 us (29%)
  matrix products  155 us (17%)
  local copies, waits for them, and re-layouts  49.2 us (5%)
  blocking collectives  42.1 us (5%)
  between operations  23.1 us (3%)
    another operation x30, other arithmetic, solve_block(): jnp.linalg.cholesky(gram_sum + damping * jnp.eye(width, dtype=gram_sum.dt...  159 us
    psum x1, waiting for transfers between devices, per_device(): gram_sum = lax.psum(local_product(feats, feats), ('wide', 'narrow'))  116 us
    ppermute x4, waiting for transfers between devices, doubled(): theirs = lax.ppermute(blocks, axis, [(i, i ^ apart) for i in range(size)])  98.1 us
    psum x1, waiting for transfers between devices, from_root(): return lax.psum(kept, axis)  95.9 us
    another operation x5, other arithmetic, solve_block(): return jax.scipy.linalg.cho_solve((factor, True), cross_sum)  80.1 us
    dot_general x2, matrix products, per_device(): jnp.dot(feats, weights, precision=lax.Precision.HIGHEST, preferred_elemen...  60.9 us
    psum x2, waiting for transfers between devices, per_device(): cross_share = lax.psum(cross_share, 'wide')  57.6 us
    dot_general x4, matrix products, local_product(): jnp.dot(left.T, right, precision=lax.Precision.HIGHEST, preferred_element...  42.5 us
  transfers between devices with their start and end apart: 10, of which 8 were waited for; matrix products, arithmetic and copies ran while one was open for 33% of the time, Pallas kernels for 0%

profile of v1, /device:TPU:0, one launch (start us, length us, event | category | flops | bytes accessed | tf_op | source)
XLA Modules:
  0.0 905.7 jit_solution(2873277519777211152)
XLA Ops:
  12.6 42.1 %all-reduce.1 = (f32[512]{0:T(512)S(1)}, f32[512]{0:T(512)S(1)}) all-reduce(f32[512]{0:T(512)S(1)} %bitcast.163, f32[512]{0:T(512)S(1)} %bitcast.162), channel_id=1, replica_groups=mesh['wide'=8,'narrow'=4] {'wide','narrow'}, use_global_device_ids=true, to_apply=%region_1.2 | all-reduce | flops 1024 | bytes 8192 | tf_op jit(solution)/shard_map/psum | solution.py:28
  54.8 95.9 %all-reduce.15.cloned.1.call-done = (f32[440,512]{1,0:T(8,128)}, f32[440,512]{1,0:T(8,128)}) async-done(((f32[440,512]{1,0:T(8,128)}, f32[440,512]{1,0:T(8,128)}), (f32[440,512]{1,0:T(8,128)}, f32[440,512]{1,0:T(8,128)})) %all-reduce.15.cloned.1.call-update) | async-done | bytes 1802256 | tf_op jit(solution)/shard_map/psum | solution.py:28
  150.7 11.2 %cosine_multiply_fusion.1 = f32[512,1024]{1,0:T(8,128)S(1)} fusion(f32[440,512]{1,0:T(8,128)} %get-tuple-element.42, f32[1024,440]{0,1:T(8,128)S(1)} %copy-done, f32[512]{0:T(512)S(1)} %get-tuple-element.38), kind=kOutput, calls=%fused_computation.12 | convolution fusion | flops 2769289216 | bytes 4802560 | tf_op jit(solution)/shard_map/dot_general | solution.py:32
  166.8 10.5 %cosine_multiply_fusion = f32[512,1024]{1,0:T(8,128)S(1)} fusion(f32[440,512]{1,0:T(8,128)S(1)} %copy-done.14, f32[1024,440]{0,1:T(8,128)S(1)} %copy-done, f32[512]{0:T(512)S(1)} %get-tuple-element.39), kind=kOutput, calls=%fused_computation.11 | convolution fusion | flops 2769289216 | bytes 4802560 | tf_op jit(solution)/shard_map/dot_general | solution.py:32
  183.3 18.0 %fusion.98 = f32[512,2048]{1,0:T(8,128)} fusion(f32[512,1024]{1,0:T(8,128)} %copy-done.5, f32[1024,2048]{1,0:T(8,128)} %param.9), kind=kOutput, calls=%fused_computation.198 | convolution fusion | flops 12884901888 | bytes 14680064 | tf_op jit(solution)/shard_map/dot_general | solution.py:39
  201.5 115.6 %all-reduce.13.cloned.1.call-done = (f32[512,512]{0,1:T(8,128)}, f32[512,512]{0,1:T(8,128)}) async-done(((f32[512,512]{0,1:T(8,128)}, f32[512,512]{0,1:T(8,128)}), (f32[512,512]{0,1:T(8,128)}, f32[512,512]{0,1:T(8,128)})) %all-reduce.13.cloned.1.call-update) | async-done | bytes 2097168 | tf_op jit(solution)/shard_map/psum | solution.py:64
  328.0 11.7 %cholesky.286 = f32[128,128]{1,0:T(8,128)S(1)} custom-call(f32[128,128]{1,0:T(8,128)S(1)} %cholesky.426), custom_call_target="Cholesky" | custom-call | tf_op jit(solution)/shard_map/jit(cholesky)/cholesky | solution.py:47
  352.2 11.7 %cholesky.305 = f32[128,128]{1,0:T(8,128)S(1)} custom-call(f32[128,128]{1,0:T(8,128)S(1)} %cholesky.430), custom_call_target="Cholesky" | custom-call | tf_op jit(solution)/shard_map/jit(cholesky)/cholesky | solution.py:47
  375.5 11.7 %cholesky.326 = f32[128,128]{1,0:T(8,128)S(1)} custom-call(f32[128,128]{1,0:T(8,128)S(1)} %cholesky.435), custom_call_target="Cholesky" | custom-call | tf_op jit(solution)/shard_map/jit(cholesky)/cholesky | solution.py:47
  398.6 12.1 %cholesky.343 = f32[128,128]{1,0:T(8,128)S(1)} custom-call(f32[128,128]{1,0:T(8,128)S(1)} %convolution_subtract_fusion.19), custom_call_target="Cholesky" | custom-call | tf_op jit(solution)/shard_map/jit(cholesky)/cholesky | solution.py:47
  417.3 11.8 %while.4 = (s32[]{:T(128)}, f32[512,512]{1,0:T(8,128)}, s32[4,2]{0,1:T(2,128)S(1)}, f32[4,128,128]{2,1,0:T(8,128)S(1)}, s32[]{:T(128)}) while((s32[]{:T(128)}, f32[512,512]{1,0:T(8,128)}, s32[4,2]{0,1:T(2,128)S(1)}, f32[4,128,128]{2,1,0:T(8,128)S(1)}, s32[]{:T(128)}) %tuple.63), condition=%wide.while_cond, body=%wide.while_body.sunk | while | flops 2 | bytes 131189 | solution.py:48
  429.1 39.3 %custom-call.32 = f32[4,128,128]{1,2,0:T(8,128)S(1)} custom-call(f32[4,128,128]{2,1,0:T(8,128)S(1)} %get-tuple-element.18), custom_call_target="InvertDiagBlocksLowerTriangular" | custom-call | tf_op jit(solution)/shard_map/jit(_cho_solve)/triangular_solve | solution.py:48
  468.5 26.6 %all-reduce.9.cloned.1.call-done = f32[512,512]{1,0:T(8,128)} async-done(((f32[512,512]{1,0:T(8,128)}), f32[512,512]{1,0:T(8,128)}) %all-reduce.9.cloned.1.call-update) | async-done | bytes 1048592 | tf_op jit(solution)/shard_map/psum | solution.py:66
  513.5 46.5 %collective-permute-done.1 = f32[2,512,512]{2,1,0:T(8,128)} collective-permute-done((f32[2,512,512]{2,1,0:T(8,128)}, f32[2,512,512]{2,1,0:T(8,128)}, u32[]{:S(2)}, u32[]{:S(2)}) %collective-permute-start.1) | collective-permute-done | bytes 2097184 | tf_op jit(solution)/shard_map/ppermute | solution.py:19
  570.2 29.9 %convolution_subtract_fusion.1 = f32[1024,2048]{1,0:T(8,128)S(1)} fusion(f32[1024,2048]{1,0:T(8,128)} %param.9, f32[512,1024]{1,0:T(8,128)} %copy-done.5, f32[512,2048]{0,1:T(8,128)} %bitcast.158), kind=kOutput, calls=%fused_computation.8 | convolution fusion | flops 12886999040 | bytes 23068672 | tf_op jit(solution)/shard_map/dot_general | solution.py:69
  603.5 15.2 %fusion.100 = f32[512,2048]{1,0:T(8,128)} fusion(f32[512,1024]{1,0:T(8,128)S(1)} %copy-done.4, f32[1024,2048]{1,0:T(8,128)S(1)} %convolution_subtract_fusion.1), kind=kOutput, calls=%fused_computation.200 | convolution fusion | flops 12884901888 | bytes 14680064 | tf_op jit(solution)/shard_map/dot_general | solution.py:39
  620.7 11.7 %cholesky.358 = f32[128,128]{1,0:T(8,128)S(1)} custom-call(f32[128,128]{1,0:T(8,128)S(1)} %cholesky.439), custom_call_target="Cholesky" | custom-call | tf_op jit(solution)/shard_map/jit(cholesky)/cholesky | solution.py:47
  644.9 11.7 %cholesky.377 = f32[128,128]{1,0:T(8,128)S(1)} custom-call(f32[128,128]{1,0:T(8,128)S(1)} %cholesky.443), custom_call_target="Cholesky" | custom-call | tf_op jit(solution)/shard_map/jit(cholesky)/cholesky | solution.py:47
  668.2 11.7 %cholesky.398 = f32[128,128]{1,0:T(8,128)S(1)} custom-call(f32[128,128]{1,0:T(8,128)S(1)} %cholesky.448), custom_call_target="Cholesky" | custom-call | tf_op jit(solution)/shard_map/jit(cholesky)/cholesky | solution.py:47
  691.2 11.7 %cholesky.415 = f32[128,128]{1,0:T(8,128)S(1)} custom-call(f32[128,128]{1,0:T(8,128)S(1)} %convolution_subtract_fusion.18), custom_call_target="Cholesky" | custom-call | tf_op jit(solution)/shard_map/jit(cholesky)/cholesky | solution.py:47
  716.7 39.3 %custom-call.36 = f32[4,128,128]{1,2,0:T(8,128)S(1)} custom-call(f32[4,128,128]{2,1,0:T(8,128)S(1)} %get-tuple-element.19), custom_call_target="InvertDiagBlocksLowerTriangular" | custom-call | tf_op jit(solution)/shard_map/jit(_cho_solve)/triangular_solve | solution.py:48
  756.0 31.0 %all-reduce.11.cloned.1.call-done = f32[512,512]{1,0:T(8,128)} async-done(((f32[512,512]{1,0:T(8,128)}), f32[512,512]{1,0:T(8,128)}) %all-reduce.11.cloned.1.call-update) | async-done | bytes 1048592 | tf_op jit(solution)/shard_map/psum | solution.py:66
  800.0 46.2 %collective-permute-done.3 = f32[2,512,512]{2,1,0:T(8,128)S(1)} collective-permute-done((f32[2,512,512]{2,1,0:T(8,128)S(1)}, f32[2,512,512]{2,1,0:T(8,128)S(1)}, u32[]{:S(2)}, u32[]{:S(2)}) %collective-permute-start.3) | collective-permute-done | bytes 2097184 | tf_op jit(solution)/shard_map/ppermute | solution.py:19
  854.4 31.0 %convolution_subtract_fusion = f32[1024,2048]{1,0:T(8,128)} fusion(f32[1024,2048]{1,0:T(8,128)} %copy-done.2, f32[512,1024]{1,0:T(8,128)} %copy-done.3, f32[512,2048]{0,1:T(8,128)} %bitcast.160), kind=kOutput, calls=%fused_computation.7 | convolution fusion | flops 12886999040 | bytes 23068672 | tf_op jit(solution)/shard_map/dot_general | solution.py:69
  (179 shorter events, 198.2 us)
Async XLA Ops:
  7.2 143.5 %copy-start = (f32[1024,440]{0,1:T(8,128)S(1)}, f32[1024,440]{0,1:T(8,128)}, u32[]{:S(2)}) copy-start(f32[1024,440]{0,1:T(8,128)} %param.8) | copy-start | bytes 5406724
  7.2 143.5 %all-reduce.15.cloned.1.call-start = ((), (), s32[]{:S(2)}) async-start(), calls=%async_computation.7 | async-start | bytes 3604480 | tf_op jit(solution)/shard_map/psum | solution.py:28
  9.9 2.7 copy-start.15
  12.6 304.5 %all-reduce.13.cloned.1.call-start = ((), (), s32[]{:S(2)}) async-start(), calls=%async_computation.6 | async-start | bytes 4194304 | tf_op jit(solution)/shard_map/psum | solution.py:64
  161.9 4.8 copy-start.5
  162.0 4.8 copy-start.14
  177.3 1.4 copy-start.3
  183.2 234.0 %reduce-scatter.3.cloned.1.call-start = ((), (), s32[]{:S(2)}) async-start(), calls=%async_computation.2 | async-start | bytes 5242880 | tf_op jit(solution)/shard_map/reduce_scatter | solution.py:65
  201.3 293.8 %all-reduce.9.cloned.1.call-start = ((), (), s32[]{:S(2)}) async-start(), calls=%async_computation.3 | async-start | bytes 2097152 | tf_op jit(solution)/shard_map/psum | solution.py:66
  417.2 291.3 %reduce-scatter.5.cloned.1.call-start = ((), (), s32[]{:S(2)}) async-start(), calls=%async_computation.4 | async-start | bytes 5242880 | tf_op jit(solution)/shard_map/reduce_scatter | solution.py:65
  429.1 69.1 %copy-start.9 = (f32[512,512]{1,0:T(8,128)S(1)}, f32[512,512]{1,0:T(8,128)}, u32[]{:S(2)}) copy-start(f32[512,512]{1,0:T(8,128)} %get-tuple-element.192) | copy-start | bytes 3145732
  468.4 35.3 %copy-start.12 = (f32[4,128,128]{1,2,0:T(8,128)}, f32[4,128,128]{1,2,0:T(8,128)S(1)}, u32[]{:S(2)}) copy-start(f32[4,128,128]{1,2,0:T(8,128)S(1)} %custom-call.32) | copy-start | bytes 786436
  506.1 2.9 collective-permute-start
  510.4 1.6 copy-start.8
  512.0 48.0 %collective-permute-start.1 = (f32[2,512,512]{2,1,0:T(8,128)}, f32[2,512,512]{2,1,0:T(8,128)}, u32[]{:S(2)}, u32[]{:S(2)}) collective-permute-start(f32[2,512,512]{2,1,0:T(8,128)} %pad_maximum_fusion.1), channel_id=1, source_target_pairs={{0,2},{1,3},{2,0},{3,1},{4,6},{5,7},{6,4},{7,5},{8,10},{9,11},{10,... | collective-permute-start | bytes 6291464 | tf_op jit(solution)/shard_map/ppermute | solution.py:19
  570.2 33.3 %copy-start.4 = (f32[512,1024]{1,0:T(8,128)S(1)}, f32[512,1024]{1,0:T(8,128)}, u32[]{:S(2)}) copy-start(f32[512,1024]{1,0:T(8,128)} %copy-done.3) | copy-start | bytes 6291460
  600.1 3.4 copy-start.2
  618.6 168.3 %all-reduce.11.cloned.1.call-start = ((), (), s32[]{:S(2)}) async-start(), calls=%async_computation.5 | async-start | bytes 2097152 | tf_op jit(solution)/shard_map/psum | solution.py:66
  787.0 3.2 copy-start.13
  795.3 2.7 collective-permute-start.2
  798.4 47.7 %collective-permute-start.3 = (f32[2,512,512]{2,1,0:T(8,128)S(1)}, f32[2,512,512]{2,1,0:T(8,128)S(1)}, u32[]{:S(2)}, u32[]{:S(2)}) collective-permute-start(f32[2,512,512]{2,1,0:T(8,128)S(1)} %pad_maximum_fusion.2), channel_id=1, source_target_pairs={{0,2},{1,3},{2,0},{3,1},{4,6},{5,7},{6,4},{7,5},{8,10},{9,11},{10,... | collective-permute-start | bytes 6291464 | tf_op jit(solution)/shard_map/ppermute | solution.py:19
  854.4 31.0 %copy-start.6 = (f32[512,4,512]{0,2,1:T(8,128)S(1)}, f32[512,4,512]{0,2,1:T(8,128)}, u32[]{:S(2)}) copy-start(f32[512,4,512]{0,2,1:T(8,128)} %copy.13) | copy-start | bytes 12582916
  854.4 31.0 %copy-start.7 = (f32[512,4,512]{0,2,1:T(8,128)S(1)}, f32[512,4,512]{0,2,1:T(8,128)}, u32[]{:S(2)}) copy-start(f32[512,4,512]{0,2,1:T(8,128)} %copy.16) | copy-start | bytes 12582916
  889.7 8.8 copy-start.1
  (2 other events, 2.1 us)
Sparse Core Ops, SparseCore 0:
  14.0 136.6 all-reduce.14
  183.4 133.7 all-reduce.12
  320.2 43.2 reduce-scatter.2
  417.4 77.6 all-reduce.8
  618.8 44.1 reduce-scatter.4
  708.7 78.2 all-reduce.10
